TPU v7x, 32 devices: a whole 2x2x4 slice. The times are simulated.
32 devices in a mesh: region: 8 (over z, y), lev: 4 (over x, core).
Axes of the slice: x: 2, y: 2, z: 4, core: 2. Of those that a mesh axis runs over, the one named last changes fastest.
Arguments:
- background_members: bfloat16 [80, 16, 1024, 8], P(None, 'lev', 'region'), may hold values from -6 to 6
- channel_height_kernel: float32 [8, 16], P(None, 'lev'), may hold values from -1.5 to 1.5
- sensor_spread_down: float32 [4], replicated, may hold values from 0.2 to 0.6
- sensor_spread_across: float32 [4], replicated, may hold values from 0.2 to 0.6
- measurement_placement: int32 [4, 64], replicated, may hold values from 0 to 511
- measurement_ordering: int32 [4, 64], replicated, may hold values from 0 to 63, each once within a row
- group_area_number: int32 [4], replicated, may hold values from 0 to 7
- taper_radius_limit: int32 [8], replicated, may hold values from 8 to 16
- measured_amounts: float32 [4, 64], replicated, may hold values from -8 to 8
- measurement_noise_spread: float32 [4, 64], replicated, may hold values from 0.05 to 0.5
Outputs:
- analysis: bfloat16 [80, 16, 8, 1024], P(None, 'lev', 'region')
All inputs are finite; a program needn't handle non-finite values.
Results may differ from a plain program's by a relative error of at most 0.001.
Values may be sent and summed in bfloat16 or wider, within the bound.
No kernel may reach another device: no remote copies, remote signals or barrier semaphores. Data moves between devices by JAX's collectives and lax.ppermute only.
A program may use at most 128 MiB of HBM per device.

v0:
```python
import jax
import jax.numpy as jnp
from jax import lax
from jax.sharding import PartitionSpec as P

TILE = 32
STRIDE = 4
highest = lax.Precision.HIGHEST
group_width = 32


def footprint(present_state_grid, sensor_spread_down, sensor_spread_across, channel_height_kernel):
    members, levels, pixels = present_state_grid.shape
    foot_cells = TILE // STRIDE
    tiles_view = present_state_grid.reshape(members, levels, foot_cells, STRIDE, foot_cells, STRIDE)
    blocks = jnp.einsum(
        "klaicj,i,j->klac", tiles_view, sensor_spread_down, sensor_spread_across, precision=highest
    )
    blocks = blocks.reshape(members, levels, foot_cells * foot_cells)
    weighted = jnp.einsum("klq,hl->khq", blocks, channel_height_kernel, precision=highest)
    return weighted.reshape(members, -1)


def taper_weight(distance, cut_radius):
    return jnp.maximum(0.0, 1.0 - distance / (cut_radius + 1.0))


def serial_block(current, values, errors):
    denominator = current.shape[0] - 1.0
    recorded = []
    for column_id in range(current.shape[1]):
        column = current[:, column_id]
        center_col = jnp.mean(column)
        anomaly_col = column - center_col
        variance = jnp.sum(anomaly_col * anomaly_col) / denominator + errors[column_id]
        alpha_gain = 1.0 / (1.0 + jnp.sqrt(errors[column_id] / variance))
        innovation = values[column_id] - center_col
        recorded.append(column)
        anomaly_all = current - jnp.mean(current, axis=0, keepdims=True)
        covariance = jnp.dot(anomaly_col, anomaly_all, precision=highest) / denominator
        current = current + jnp.outer(innovation - alpha_gain * anomaly_col, covariance / variance)
    return jnp.stack(recorded, axis=1)


def block_terms(recorded, values, errors):
    denominator = recorded.shape[0] - 1.0
    center_blk = jnp.mean(recorded, axis=0)
    anomaly_rec = recorded - center_blk[None]
    variance = jnp.sum(anomaly_rec * anomaly_rec, axis=0) / denominator + errors
    alpha_gain = 1.0 / (1.0 + jnp.sqrt(errors / variance))
    scale_pert = alpha_gain / (denominator * variance)
    scale_mean = (values - center_blk) / (denominator * variance)
    return (anomaly_rec, scale_pert, scale_mean)


def advance(transforms, offsets, anomaly_rec, scale_pert, scale_mean, tapers):
    block_size = anomaly_rec.shape[1]
    gram_matrix = jnp.dot(anomaly_rec.T, anomaly_rec, precision=highest)
    upper_part = jnp.triu(gram_matrix, 1)
    coef_pert = tapers * scale_pert[None]
    coef_mean = tapers * scale_mean[None]
    identity_blk = jnp.eye(block_size, dtype=jnp.float32)[None]
    nilpotent = coef_pert[:, :, None] * upper_part[None]
    inverse = identity_blk - nilpotent
    power = nilpotent
    for level_id in range((block_size - 1).bit_length() - 1):
        power = jnp.einsum("tij,tjk->tik", power, power, precision=highest)
        inverse = inverse + jnp.einsum("tij,tjk->tik", inverse, power, precision=highest)
    factor = inverse * coef_pert[:, None, :]
    carried = jnp.einsum("ij,tj->ti", upper_part, coef_mean, precision=highest)
    weights_mean = coef_mean - jnp.einsum("tij,tj->ti", factor, carried, precision=highest)
    mapped = jnp.einsum("tkm,mj->tkj", transforms, anomaly_rec, precision=highest)
    offsets = offsets + jnp.einsum("tkj,tj->tk", mapped, weights_mean, precision=highest)
    folded = jnp.einsum("tkj,tjl->tkl", mapped, factor, precision=highest)
    transforms = transforms - jnp.einsum("tkl,ml->tkm", folded, anomaly_rec, precision=highest)
    return (transforms, offsets)


def run_batch(base_priors, values, errors, transforms, offsets, tapers, target):
    center = jnp.mean(base_priors, axis=0)
    anomaly = base_priors - center[None]
    count_blocks = base_priors.shape[1] // group_width

    def one_block(block_id, state_carry):
        transforms, offsets, recorded_all = state_carry
        start = block_id * group_width
        anomaly_blk = lax.dynamic_slice_in_dim(anomaly, start, group_width, 1)
        center_blk = lax.dynamic_slice_in_dim(center, start, group_width, 0)
        values_blk = lax.dynamic_slice_in_dim(values, start, group_width, 0)
        errors_blk = lax.dynamic_slice_in_dim(errors, start, group_width, 0)
        tapers_blk = lax.dynamic_slice_in_dim(tapers, start, group_width, 1)
        current = (
            jnp.dot(transforms[target].T, anomaly_blk, precision=highest)
            + (center_blk + jnp.dot(offsets[target], anomaly_blk, precision=highest))[None]
        )
        recorded = serial_block(current, values_blk, errors_blk)
        anomaly_rec, scale_pert, scale_mean = block_terms(recorded, values_blk, errors_blk)
        transforms, offsets = advance(
            transforms, offsets, anomaly_rec, scale_pert, scale_mean, tapers_blk
        )
        recorded_all = lax.dynamic_update_slice_in_dim(recorded_all, recorded, start, 1)
        return (transforms, offsets, recorded_all)

    return lax.fori_loop(
        0, count_blocks, one_block, (transforms, offsets, jnp.zeros_like(base_priors))
    )


def body(
    background_members,
    channel_height_kernel,
    sensor_spread_down,
    sensor_spread_across,
    measurement_placement,
    measurement_ordering,
    group_area_number,
    taper_radius_limit,
    measured_amounts,
    measurement_noise_spread,
):
    own_region = lax.axis_index("region")
    present_state_grid = lax.all_to_all(
        background_members, "region", split_axis=3, concat_axis=2, tiled=True
    )[:, :, :, 0].astype(jnp.float32)
    present_state_grid, partial_priors = (
        present_state_grid,
        footprint(
            present_state_grid, sensor_spread_down, sensor_spread_across, channel_height_kernel
        ),
    )
    priors = lax.psum(partial_priors, "lev")
    members, levels, pixels = present_state_grid.shape
    flat_field = present_state_grid.reshape(members, levels * pixels)
    center = jnp.mean(flat_field, axis=0)
    anomaly = flat_field - center[None]
    picked = jnp.take_along_axis(measurement_placement, measurement_ordering, axis=1)
    values_all = jnp.take_along_axis(measured_amounts, measurement_ordering, axis=1)
    errors_all = jnp.take_along_axis(measurement_noise_spread, measurement_ordering, axis=1)
    foot_cells = TILE // STRIDE * (TILE // STRIDE)
    channels = picked // foot_cells
    channel_ids = jnp.arange(taper_radius_limit.shape[0], dtype=jnp.int32)
    cut_radius = jnp.sum(
        jnp.where(channels[:, :, None] == channel_ids, taper_radius_limit, 0), axis=2
    ).astype(jnp.float32)
    batches = measurement_placement.shape[0]
    eye_members = jnp.eye(members, dtype=jnp.float32)
    hosting = own_region == group_area_number
    chosen = jnp.take(priors, picked.reshape(-1), axis=1).reshape(members, batches, -1)
    chosen = jnp.where(hosting[None, :, None], chosen, 0.0)
    bases = lax.psum(chosen, "region")
    targets = jnp.concatenate([own_region[None], group_area_number])
    count_targets = batches + 1
    transforms = jnp.tile(eye_members[None], (count_targets, 1, 1))
    offsets = jnp.zeros((count_targets, members), jnp.float32)
    for batch_id in range(batches):
        distance = jnp.abs(targets - group_area_number[batch_id]).astype(jnp.float32)
        tapers = taper_weight(distance[:, None], cut_radius[batch_id][None])
        outcome = run_batch(
            bases[:, batch_id],
            values_all[batch_id],
            errors_all[batch_id],
            transforms,
            offsets,
            tapers,
            1 + batch_id,
        )
        transforms, offsets = (outcome[0], outcome[1])
    mixing = transforms[0] + offsets[0][:, None]
    result = jnp.dot(mixing.T, anomaly, precision=highest) + center[None]
    return result.reshape(members, levels, 1, pixels).astype(jnp.bfloat16)


def solution(mesh):
    return jax.shard_map(
        body,
        mesh=mesh,
        in_specs=(
            P(None, "lev", "region", None),
            P(None, "lev"),
            P(),
            P(),
            P(),
            P(),
            P(),
            P(),
            P(),
            P(),
        ),
        out_specs=P(None, "lev", "region", None),
        check_vma=False,
    )
```

profile of v0, /device:TPU:0, one launch (start us, length us, event | category | flops | bytes accessed | tf_op | source)
XLA Modules:
  0.0 1444.8 jit_solution(3757707560450293175)
XLA Ops:
  6.5 2.2 copy.48
  8.8 7.5 all-to-all-start
  16.4 2.4 gather_fusion.1
  19.8 0.7 abs_convert_fusion
  20.6 1.8 abs_convert_fusion.1
  22.5 2.4 gather_fusion.3
  25.1 2.4 gather_fusion.2
  27.8 5.8 all-to-all-done
  33.5 0.7 copy.49
  34.9 0.9 multiply_reduce_fusion.4
  36.2 0.8 copy.84
  37.4 31.1 %all-reduce.3.cloned.1.call-done = f32[80,512]{0,1:T(8,128)} async-done(((f32[80,512]{0,1:T(8,128)}), f32[80,512]{0,1:T(8,128)}) %all-reduce.3.cloned.1.call-update) | async-done | bytes 163856 | tf_op jit(solution)/shard_map/psum | solution.py:131
  68.5 1.7 gather_fusion
  70.2 0.7 select_select_fusion
  71.8 1.8 copy.54
  73.6 1.5 sub.8074
  75.1 66.7 %all-reduce.5.cloned.1.call-done = f32[80,4,64]{2,0,1:T(8,128)} async-done(((f32[80,4,64]{2,0,1:T(8,128)}), f32[80,4,64]{2,0,1:T(8,128)}) %all-reduce.5.cloned.1.call-update) | async-done | bytes 81936 | tf_op jit(solution)/shard_map/psum | solution.py:150
  141.8 0.9 slice_reduce_fusion.124
  142.7 0.9 bitcast_subtract_fusion.4
  143.6 322.7 %while.64 = (s32[]{:T(128)}, f32[5,80,80]{2,1,0:T(8,128)S(1)}, f32[5,80]{1,0:T(8,128)S(1)}, f32[80,64]{1,0:T(8,128)S(1)}, f32[64]{0:T(128)S(1)}, /*index=5*/f32[...) while((s32[]{:T(128)}, f32[5,80,80]{2,1,0:T(8,128)S(1)}, ...), condition=%wide.region_100.102_spmd.clone, body=%wide.region_4.101_spmd.clone.sunk | while | flops 50354160 | bytes 2541750 | solution.py:104
  144.0 0.7 fusion.2380
  144.7 0.7 fusion.2376
  145.4 0.7 fusion.2414
  146.1 0.7 fusion.2418
  191.3 0.7 slice_reduce_fusion.354
  305.3 0.7 fusion.2380
  306.0 0.7 fusion.2376
  306.7 0.7 fusion.2414
  307.5 0.7 fusion.2418
  352.6 0.7 slice_reduce_fusion.354
  466.3 323.2 %while.61 = (s32[]{:T(128)}, f32[5,80,80]{2,1,0:T(8,128)S(1)}, f32[5,80]{1,0:T(8,128)S(1)}, f32[80,64]{1,0:T(8,128)S(1)}, f32[64]{0:T(128)S(1)}, /*index=5*/f32[...) while((s32[]{:T(128)}, f32[5,80,80]{2,1,0:T(8,128)S(1)}, ...), condition=%wide.region_198.200_spmd, body=%wide.region_102.199_spmd.sunk | while | flops 50353360 | bytes 2538531 | solution.py:104
  467.2 0.7 fusion.1876
  467.9 0.7 fusion.1872
  468.6 0.7 fusion.1910
  469.3 0.7 fusion.1914
  514.5 0.7 slice_reduce_fusion.261
  628.5 0.7 fusion.1876
  629.2 0.7 fusion.1872
  629.9 0.7 fusion.1910
  630.6 0.7 fusion.1914
  675.8 0.7 slice_reduce_fusion.261
  789.5 322.8 %while.62 = (s32[]{:T(128)}, f32[5,80,80]{2,1,0:T(8,128)S(1)}, f32[5,80]{1,0:T(8,128)S(1)}, f32[80,64]{1,0:T(8,128)S(1)}, f32[64]{0:T(128)S(1)}, /*index=5*/f32[...) while((s32[]{:T(128)}, f32[5,80,80]{2,1,0:T(8,128)S(1)}, ...), condition=%wide.region_296.298_spmd, body=%wide.region_200.297_spmd.sunk | while | flops 50353360 | bytes 2538531 | solution.py:104
  790.0 0.7 fusion.2044
  790.7 0.7 fusion.2040
  791.4 0.7 fusion.2078
  792.1 0.7 fusion.2082
  837.3 0.7 slice_reduce_fusion.292
  951.3 0.7 fusion.2044
  952.0 0.7 fusion.2040
  952.7 0.7 fusion.2078
  953.4 0.7 fusion.2082
  998.6 0.7 slice_reduce_fusion.292
  1112.3 322.9 %while.63 = (s32[]{:T(128)}, f32[5,80,80]{2,1,0:T(8,128)S(1)}, f32[5,80]{1,0:T(8,128)S(1)}, f32[80,64]{1,0:T(8,128)S(1)}, f32[64]{0:T(128)S(1)}, /*index=5*/f32[...) while((s32[]{:T(128)}, f32[5,80,80]{2,1,0:T(8,128)S(1)}, ...), condition=%wide.region_394.396_spmd, body=%wide.region_298.395_spmd.sunk | while | flops 50353360 | bytes 2538531 | solution.py:104
  1112.9 0.7 fusion.2212
  1113.6 0.7 fusion.2208
  1114.3 0.7 fusion.2246
  1115.0 0.7 fusion.2250
  1160.1 0.7 slice_reduce_fusion.323
  1274.2 0.7 fusion.2212
  1274.9 0.7 fusion.2208
  1275.6 0.7 fusion.2246
  1276.3 0.7 fusion.2250
  1435.1 1.3 fusion.888
  1436.5 1.3 convert_element_type.110
  (1770 shorter events, 457.7 us)
Async XLA Ops:
  6.5 29.2 %copy-start = (f32[8,4]{0,1:T(4,128)S(1)}, f32[8,4]{0,1:T(4,128)}, u32[]{:S(2)}) copy-start(f32[8,4]{0,1:T(4,128)} %param.21) | copy-start | bytes 388
  6.5 9.8 copy-start.5
  6.5 9.9 copy-start.1
  8.8 10.3 copy-start.4
  8.8 11.0 copy-start.7
  8.8 11.0 copy-start.8
  8.8 11.7 copy-start.6
  8.8 13.8 copy-start.2
  8.8 24.7 %all-to-all-start = ((bf16[80,4,128,8]{2,0,1,3:T(8,128)(2,1)}), bf16[80,4,128,8]{2,0,1,3:T(8,128)(2,1)S(1)}, u32[]{:S(2)}, u32[]{:S(2)}) async-start(bf16[80,4,128,8]{2,0,1,3:T(8,128)(2,1)} %copy.48), calls=%async_computation | async-start | bytes 1310720 | tf_op jit(solution)/shard_map/all_to_all | solution.py:122
  16.2 52.2 %all-reduce.3.cloned.1.call-start = ((), (), s32[]{:S(2)}) async-start(), calls=%async_computation.1 | async-start | bytes 524288 | tf_op jit(solution)/shard_map/psum | solution.py:131
  16.4 8.7 copy-start.3
  37.0 104.8 %all-reduce.5.cloned.1.call-start = ((), (), s32[]{:S(2)}) async-start(), calls=%async_computation.2 | async-start | bytes 327680 | tf_op jit(solution)/shard_map/psum | solution.py:150
Sparse Core Ops, SparseCore 0:
  37.1 31.3 all-reduce.2
  71.8 69.9 all-reduce.4
where the time goes:
time: 1460 us; the launch traced here: 1440 us
  loops' own time  810 us (55%)
  other arithmetic  372 us (25%)
  waiting for transfers between devices  104 us (7%)
  matrix products  88.7 us (6%)
  local copies, waits for them, and re-layouts  48.2 us (3%)
    another operation x4, loops' own time, run_batch(): lax.fori_loop(0, count_blocks, one_block, (transforms, offsets, jnp.zeros...  810 us
    reduce_sum x248, other arithmetic, serial_block(): center_col = jnp.mean(column)  154 us
    reduce_sum x248, other arithmetic, serial_block(): jnp.sum(anomaly_col * anomaly_col) / denominator + errors[column_id]  153 us
    psum x1, waiting for transfers between devices, body(): bases = lax.psum(chosen, 'region')  66.7 us
    dot_general x248, matrix products, serial_block(): jnp.dot(anomaly_col, anomaly_all, precision=highest) / denominator  49.4 us
    reduce_sum x240, other arithmetic, serial_block(): anomaly_all = current - jnp.mean(current, axis=0, keepdims=True)  43.3 us
    psum x1, waiting for transfers between devices, body(): priors = lax.psum(partial_priors, 'lev')  31.1 us
  transfers between devices with their start and end apart: 3, of which 3 were waited for; matrix products, arithmetic and copies ran while one was open for 1% of the time, Pallas kernels for 0%

commit v1 on v0

--- a/solution.py
+++ b/solution.py
@@ -147,7 +147,7 @@
     hosting = own_region == group_area_number
     chosen = jnp.take(priors, picked.reshape(-1), axis=1).reshape(members, batches, -1)
     chosen = jnp.where(hosting[None, :, None], chosen, 0.0)
-    bases = lax.psum(chosen, "region")
+    bases = jnp.sum(lax.all_gather(chosen, "region"), axis=0)
     targets = jnp.concatenate([own_region[None], group_area_number])
     count_targets = batches + 1
     transforms = jnp.tile(eye_members[None], (count_targets, 1, 1))

time: 1460 us -> 1420 us (0.973)
  waiting for transfers between devices: 104 us -> 33.1 us
  blocking collectives: 0 us -> 34 us
    psum x1 -> x0, waiting for transfers between devices: 66.7 us -> none  [body(): bases = lax.psum(chosen, 'region')]
    all_gather x0 -> x1, blocking collectives: none -> 34 us  [body(): bases = jnp.sum(lax.all_gather(chosen, 'region'), axis=0)]
  transfers between devices with their start and end apart: 3 -> 2, of which waited for: 3 -> 2; matrix products, arithmetic and copies ran while one was open for 1% -> 1% of each run, Pallas kernels for 0% -> 0%
where the time goes in v1:
time: 1420 us; the launch traced here: 1400 us
  loops' own time  810 us (57%)
  other arithmetic  370 us (26%)
  matrix products  86.6 us (6%)
  local copies, waits for them, and re-layouts  48.4 us (3%)
  blocking collectives  34 us (2%)
  waiting for transfers between devices  33.1 us (2%)
    another operation x4, loops' own time, run_batch(): lax.fori_loop(0, count_blocks, one_block, (transforms, offsets, jnp.zeros...  810 us
    reduce_sum x248, other arithmetic, serial_block(): center_col = jnp.mean(column)  154 us
    reduce_sum x248, other arithmetic, serial_block(): jnp.sum(anomaly_col * anomaly_col) / denominator + errors[column_id]  153 us
    dot_general x248, matrix products, serial_block(): jnp.dot(anomaly_col, anomaly_all, precision=highest) / denominator  49.4 us
    reduce_sum x240, other arithmetic, serial_block(): anomaly_all = current - jnp.mean(current, axis=0, keepdims=True)  43.3 us
    all_gather x1, blocking collectives, body(): bases = jnp.sum(lax.all_gather(chosen, 'region'), axis=0)  34 us
  transfers between devices with their start and end apart: 2, of which 2 were waited for; matrix products, arithmetic and copies ran while one was open for 1% of the time, Pallas kernels for 0%

profile of v1, /device:TPU:0, one launch (start us, length us, event | category | flops | bytes accessed | tf_op | source)
XLA Modules:
  0.0 1404.2 jit_solution(8630704788993952812)
XLA Ops:
  6.5 2.2 copy.48
  8.8 7.5 all-to-all-start
  16.4 2.4 gather_fusion.1
  19.8 0.7 abs_convert_fusion
  20.6 1.8 abs_convert_fusion.1
  22.5 2.4 gather_fusion.3
  25.1 2.4 gather_fusion.2
  27.8 5.8 all-to-all-done
  33.5 0.7 copy.49
  34.9 0.9 multiply_reduce_fusion.4
  36.2 0.8 copy.87
  37.8 1.8 copy.57
  39.6 1.5 sub.8074
  41.1 27.4 %all-reduce.2.cloned.1.call-done = f32[80,512]{0,1:T(8,128)} async-done(((f32[80,512]{0,1:T(8,128)}), f32[80,512]{0,1:T(8,128)}) %all-reduce.2.cloned.1.call-update) | async-done | bytes 163856 | tf_op jit(solution)/shard_map/psum | solution.py:131
  68.5 1.7 gather_fusion
  70.3 34.0 %all_gather.4 = f32[8,80,4,64]{1,3,2,0:T(8,128)S(1)} all-gather(f32[1,80,4,64]{1,3,2,0:T(8,128)S(1)} %select_select_fusion), channel_id=1, replica_groups=mesh['region'=8,'lev'=4] {'region'}, dimensions={0}, use_global_device_ids=true | all-gather | bytes 737280 | tf_op jit(solution)/shard_map/all_gather | solution.py:150
  104.7 322.2 %while.64 = (s32[]{:T(128)}, f32[5,80,80]{2,1,0:T(8,128)S(1)}, f32[5,80]{1,0:T(8,128)S(1)}, f32[80,64]{0,1:T(8,128)S(1)}, f32[64]{0:T(128)S(1)}, /*index=5*/f32[...) while((s32[]{:T(128)}, f32[5,80,80]{2,1,0:T(8,128)S(1)}, ...), condition=%wide.region_100.102_spmd.clone, body=%wide.region_4.101_spmd.clone.sunk | while | flops 50354160 | bytes 2492598 | solution.py:104
  105.0 0.7 fusion.2380
  105.7 0.7 fusion.2376
  106.4 0.7 fusion.2414
  107.1 0.7 fusion.2418
  137.6 0.7 slice_reduce_fusion.351
  152.1 0.7 slice_reduce_fusion.354
  266.1 0.7 fusion.2380
  266.8 0.7 fusion.2376
  267.5 0.7 fusion.2414
  268.2 0.7 fusion.2418
  313.2 0.7 slice_reduce_fusion.354
  426.9 322.7 %while.61 = (s32[]{:T(128)}, f32[5,80,80]{2,1,0:T(8,128)S(1)}, f32[5,80]{1,0:T(8,128)S(1)}, f32[80,64]{0,1:T(8,128)S(1)}, f32[64]{0:T(128)S(1)}, /*index=5*/f32[...) while((s32[]{:T(128)}, f32[5,80,80]{2,1,0:T(8,128)S(1)}, ...), condition=%wide.region_198.200_spmd, body=%wide.region_102.199_spmd.sunk | while | flops 50353360 | bytes 2489379 | solution.py:104
  427.7 0.7 fusion.1876
  428.4 0.7 fusion.1872
  429.1 0.7 fusion.1910
  429.9 0.7 fusion.1914
  474.9 0.7 slice_reduce_fusion.261
  588.8 0.7 fusion.1876
  589.5 0.7 fusion.1872
  590.2 0.7 fusion.1910
  591.0 0.7 fusion.1914
  636.0 0.7 slice_reduce_fusion.261
  749.7 322.4 %while.62 = (s32[]{:T(128)}, f32[5,80,80]{2,1,0:T(8,128)S(1)}, f32[5,80]{1,0:T(8,128)S(1)}, f32[80,64]{0,1:T(8,128)S(1)}, f32[64]{0:T(128)S(1)}, /*index=5*/f32[...) while((s32[]{:T(128)}, f32[5,80,80]{2,1,0:T(8,128)S(1)}, ...), condition=%wide.region_296.298_spmd, body=%wide.region_200.297_spmd.sunk | while | flops 50353360 | bytes 2489379 | solution.py:104
  750.1 0.7 fusion.2044
  750.8 0.7 fusion.2040
  751.5 0.7 fusion.2078
  752.3 0.7 fusion.2082
  797.3 0.7 slice_reduce_fusion.292
  911.2 0.7 fusion.2044
  911.9 0.7 fusion.2040
  912.6 0.7 fusion.2078
  913.4 0.7 fusion.2082
  958.4 0.7 slice_reduce_fusion.292
  1072.0 322.4 %while.63 = (s32[]{:T(128)}, f32[5,80,80]{2,1,0:T(8,128)S(1)}, f32[5,80]{1,0:T(8,128)S(1)}, f32[80,64]{0,1:T(8,128)S(1)}, f32[64]{0:T(128)S(1)}, /*index=5*/f32[...) while((s32[]{:T(128)}, f32[5,80,80]{2,1,0:T(8,128)S(1)}, ...), condition=%wide.region_394.396_spmd, body=%wide.region_298.395_spmd.sunk | while | flops 50353360 | bytes 2489379 | solution.py:104
  1072.5 0.7 fusion.2212
  1073.3 0.7 fusion.2208
  1073.9 0.7 fusion.2246
  1074.7 0.7 fusion.2250
  1119.7 0.7 slice_reduce_fusion.323
  1233.6 0.7 fusion.2212
  1234.3 0.7 fusion.2208
  1235.0 0.7 fusion.2246
  1235.8 0.7 fusion.2250
  1266.2 0.7 slice_reduce_fusion.320
  1280.8 0.7 slice_reduce_fusion.323
  1394.5 1.3 fusion.888
  1395.8 1.3 convert_element_type.110
  (1768 shorter events, 453.6 us)
Async XLA Ops:
  6.5 29.2 %copy-start = (f32[8,4]{0,1:T(4,128)S(1)}, f32[8,4]{0,1:T(4,128)}, u32[]{:S(2)}) copy-start(f32[8,4]{0,1:T(4,128)} %param.21) | copy-start | bytes 388
  6.5 9.8 copy-start.5
  6.5 9.9 copy-start.1
  8.8 10.3 copy-start.4
  8.8 11.0 copy-start.7
  8.8 11.0 copy-start.8
  8.8 11.7 copy-start.6
  8.8 13.8 copy-start.2
  8.8 24.7 %all-to-all-start = ((bf16[80,4,128,8]{2,0,1,3:T(8,128)(2,1)}), bf16[80,4,128,8]{2,0,1,3:T(8,128)(2,1)S(1)}, u32[]{:S(2)}, u32[]{:S(2)}) async-start(bf16[80,4,128,8]{2,0,1,3:T(8,128)(2,1)} %copy.48), calls=%async_computation | async-start | bytes 1310720 | tf_op jit(solution)/shard_map/all_to_all | solution.py:122
  16.2 52.2 %all-reduce.2.cloned.1.call-start = ((), (), s32[]{:S(2)}) async-start(), calls=%async_computation.1 | async-start | bytes 524288 | tf_op jit(solution)/shard_map/psum | solution.py:131
  16.4 8.7 copy-start.3
Sparse Core Ops, SparseCore 0:
  37.1 31.3 all-reduce.1
